TPU v7x, 32 devices: a whole 2x2x4 slice. The times are simulated.
32 devices in a mesh: row: 2 (over y), col: 16 (over z, x, core).
Axes of the slice: x: 2, y: 2, z: 4, core: 2. Of those that a mesh axis runs over, the one named last changes fastest.
Arguments:
- queries: bfloat16 [8192, 1024], P(('row', 'col')), may hold values from -8 to 8
- key_rows: bfloat16 [8192, 1024], P(('row', 'col')), may hold values from -8 to 8
- value_rows: bfloat16 [8192, 1024], P(('row', 'col')), may hold values from -6 to 6
- out_grad: bfloat16 [8192, 1024], P(('row', 'col')), may hold values from -6 to 6
- dropout_bits: int32 [8192, 128], P(('row', 'col')), may hold values from 0 to 255, as said below
- partner: int32 [3, 2, 16], replicated, may hold values from 0 to 15, each once within a row
- block_pick: int32 [3, 2, 16], replicated, may hold values from 0 to 1
- global_blocks: int32 [2], replicated, may hold values from 0 to 63
Outputs:
- attended: bfloat16 [8192, 1024], P(('row', 'col'))
- query_grad: bfloat16 [8192, 1024], P(('row', 'col'))
- key_grad: bfloat16 [8192, 1024], P(('row', 'col'))
- value_grad: bfloat16 [8192, 1024], P(('row', 'col'))
Inputs may be any that keep to these rules, and one draw needn't show every extreme that they name: `dropout_bits`: each word packs 8 flags of 0 or 1 in its low bits. partner[r, a, :] is a permutation of the places 0 to 15.
All inputs are finite; a program needn't handle non-finite values.
Results may differ from a plain program's by a relative error of at most 0.0085.
Values may be sent and summed in bfloat16 or wider, within the bound.
A program may use at most 128 MiB of HBM per device.

v0:
```python
import functools

import jax
import jax.numpy as jnp
from jax import lax
from jax.experimental import pallas as pl
from jax.experimental.pallas import tpu as pltpu
from jax.sharding import PartitionSpec as P

HEADS = 16
HEAD_DIM = 64
BLOCK = 128
NGLOBAL = 2
NMATCH = 3
PAIR = 2 * HEAD_DIM
SLOTS = 3 + NGLOBAL + NMATCH
CHUNKS = 1

score_scale = 0.125
keep_scale = 1.0 / 0.9


def contract(a, b, dim_a, dim_b):
    return lax.dot_general(a, b, (((dim_a,), (dim_b,)), ((), ())), preferred_element_type=jnp.float32)


def attention_kernel(
    blocks, q_ref, g_ref, ko_ref, vo_ref, kp_ref, vp_ref, kn_ref, vn_ref, kg_ref, vg_ref, kr_ref, vr_ref, bits_ref,
    att_ref, qg_ref, own_ref, rims_ref, far_ref,
    keep_ref, kall_ref, vall_ref, qall_ref, gall_ref, s_ref, dp_ref, p_ref, ds_ref,
):
    near = blocks + 2
    own_rows = blocks * BLOCK

    @pl.when(pl.program_id(0) == 0)
    def _():
        shifts = lax.broadcasted_iota(jnp.int32, (BLOCK // 8, 8, BLOCK), 1)
        for j in range(blocks):
            for i in range(SLOTS):
                words = bits_ref[j, i * BLOCK // 8 : (i + 1) * BLOCK // 8, :]
                flags = jnp.right_shift(jnp.broadcast_to(words[:, None, :], shifts.shape), shifts) & 1
                keep_ref[j, i] = (flags.astype(jnp.float32) * keep_scale).reshape(BLOCK, BLOCK)
        p_ref[...] = jnp.zeros_like(p_ref)
        ds_ref[...] = jnp.zeros_like(ds_ref)

    for all_ref, parts in ((kall_ref, (kp_ref, ko_ref, kn_ref, kg_ref, kr_ref)), (vall_ref, (vp_ref, vo_ref, vn_ref, vg_ref, vr_ref))):
        row = 0
        for part in parts:
            all_ref[row : row + part.shape[0], :] = part[...]
            row += part.shape[0]
    first = lax.broadcasted_iota(jnp.int32, (BLOCK, PAIR), 1) < HEAD_DIM
    zero = jnp.zeros((BLOCK, PAIR), jnp.bfloat16)
    for j in range(blocks):
        rows = slice(j * BLOCK, (j + 1) * BLOCK)
        query = (q_ref[rows, :].astype(jnp.float32) * score_scale).astype(jnp.bfloat16)
        grad = g_ref[rows, :]
        base = 2 * j * BLOCK
        qall_ref[base : base + BLOCK, :] = jnp.where(first, query, zero)
        qall_ref[base + BLOCK : base + 2 * BLOCK, :] = jnp.where(first, zero, query)
        gall_ref[base : base + BLOCK, :] = jnp.where(first, grad, zero)
        gall_ref[base + BLOCK : base + 2 * BLOCK, :] = jnp.where(first, zero, grad)

    wide = 2 * BLOCK
    for j in range(blocks):
        cols = slice(j * wide, (j + 1) * wide)
        places = [j, j + 1, j + 2] + list(range(near, near + NGLOBAL + NMATCH))
        query = qall_ref[cols, :]
        grad = gall_ref[cols, :]
        top = None
        for i, b in enumerate(places):
            score = contract(kall_ref[b * BLOCK : (b + 1) * BLOCK, :], query, 1, 1)
            s_ref[i] = score
            part = jnp.max(score.reshape(BLOCK // 8, 8, wide), axis=0)
            top = part if top is None else jnp.maximum(top, part)
        top = jnp.max(top, axis=0, keepdims=True)
        total, mixed = None, None
        for i, b in enumerate(places):
            keep = keep_ref[j, i]
            keep = jnp.concatenate([keep, keep], axis=1)
            weight = jnp.exp(s_ref[i] - top)
            s_ref[i] = weight
            grad_p = contract(vall_ref[b * BLOCK : (b + 1) * BLOCK, :], grad, 1, 1) * keep
            dp_ref[i] = grad_p
            part = jnp.sum(weight.reshape(BLOCK // 8, 8, wide), axis=0)
            cross = jnp.sum((weight * grad_p).reshape(BLOCK // 8, 8, wide), axis=0)
            total = part if total is None else total + part
            mixed = cross if mixed is None else mixed + cross
        inverse = 1.0 / jnp.sum(total, axis=0, keepdims=True)
        delta = jnp.sum(mixed, axis=0, keepdims=True) * inverse
        for i, b in enumerate(places):
            keep = keep_ref[j, i]
            keep = jnp.concatenate([keep, keep], axis=1)
            probs = s_ref[i] * inverse
            p_ref[b * BLOCK : (b + 1) * BLOCK, cols] = (probs * keep).astype(jnp.bfloat16)
            ds_ref[b * BLOCK : (b + 1) * BLOCK, cols] = (probs * (dp_ref[i] - delta)).astype(jnp.bfloat16)

    out_t = contract(vall_ref[...], p_ref[...], 0, 0)
    qg_t = contract(kall_ref[...], ds_ref[...], 0, 0) * score_scale
    for j in range(blocks):
        rows = slice(j * BLOCK, (j + 1) * BLOCK)
        base = j * wide
        for result, ref in ((out_t, att_ref), (qg_t, qg_ref)):
            picked = jnp.concatenate(
                [result[:HEAD_DIM, base : base + BLOCK], result[HEAD_DIM:, base + BLOCK : base + wide]], axis=0
            )
            ref[rows, :] = picked.T.astype(jnp.bfloat16)
    for which, (left, right) in enumerate(((ds_ref, qall_ref), (p_ref, gall_ref))):
        grads = contract(left[...], right[...], 1, 0)
        own_ref[which] = grads[BLOCK : BLOCK + own_rows]
        rims_ref[which, :BLOCK] = grads[:BLOCK].astype(jnp.bfloat16)
        rims_ref[which, BLOCK:] = grads[BLOCK + own_rows : near * BLOCK].astype(jnp.bfloat16)
        far_ref[which] = grads[near * BLOCK :].astype(jnp.bfloat16)


def attention(queries, out_grad, key_rows, value_rows, before, after, shared, fetched, bits, chunk):
    tokens_here, width = queries.shape
    blocks = tokens_here // BLOCK
    pairs = width // PAIR // CHUNKS
    start = chunk * pairs
    part_width = width // CHUNKS
    far_rows = (NGLOBAL + NMATCH) * BLOCK
    all_rows = (blocks + 2) * BLOCK + far_rows

    def plain(rows):
        return pl.BlockSpec((rows, PAIR), lambda h: (0, start + h))

    def halves(rows):
        return [pl.BlockSpec((rows, PAIR), lambda h: (0, h)), pl.BlockSpec((rows, PAIR), lambda h: (0, pairs + h))]

    def out(rows, kind):
        return pl.BlockSpec((2, rows, PAIR), lambda h: (0, 0, h)), jax.ShapeDtypeStruct((2, rows, part_width), kind)

    flat = pl.BlockSpec((tokens_here, PAIR), lambda h: (0, h)), jax.ShapeDtypeStruct((tokens_here, part_width), jnp.bfloat16)
    outs = [flat, flat, out(tokens_here, jnp.float32), out(2 * BLOCK, jnp.bfloat16), out(far_rows, jnp.bfloat16)]
    pair_work = HEADS // CHUNKS * tokens_here * SLOTS * BLOCK
    return pl.pallas_call(
        functools.partial(attention_kernel, blocks),
        grid=(pairs,),
        in_specs=[plain(tokens_here)] * 4
        + halves(BLOCK) + halves(BLOCK) + halves(NGLOBAL * BLOCK) + halves(NMATCH * BLOCK)
        + [pl.BlockSpec(bits.shape, lambda h: (0, 0, 0))],
        out_specs=[spec for spec, _ in outs],
        out_shape=[shape for _, shape in outs],
        scratch_shapes=[
            pltpu.VMEM((blocks, SLOTS, BLOCK, BLOCK), jnp.float32),
            pltpu.VMEM((all_rows, PAIR), jnp.bfloat16),
            pltpu.VMEM((all_rows, PAIR), jnp.bfloat16),
            pltpu.VMEM((2 * tokens_here, PAIR), jnp.bfloat16),
            pltpu.VMEM((2 * tokens_here, PAIR), jnp.bfloat16),
            pltpu.VMEM((SLOTS, BLOCK, 2 * BLOCK), jnp.float32),
            pltpu.VMEM((SLOTS, BLOCK, 2 * BLOCK), jnp.float32),
            pltpu.VMEM((all_rows, 2 * tokens_here), jnp.bfloat16),
            pltpu.VMEM((all_rows, 2 * tokens_here), jnp.bfloat16),
        ],
        cost_estimate=pl.CostEstimate(
            flops=pair_work * HEAD_DIM * 2 * 7, bytes_accessed=16 * tokens_here * part_width, transcendentals=pair_work
        ),
        name="block_attention",
    )(queries, out_grad, key_rows, value_rows, before, before, after, after, shared, shared, fetched, fetched, bits)


def partner_of(me, bit):
    flag = (me // 2**bit) % 2
    return flag, me + 2**bit - 2 * 2**bit * flag


def greet(me, cols):
    barrier = pltpu.get_barrier_semaphore()

    def hello(step, carry):
        pl.semaphore_signal(barrier, inc=1, device_id={"col": (me + step) % cols})
        return carry

    lax.fori_loop(1, cols, hello, 0)
    pl.semaphore_wait(barrier, cols - 1)


def bulk_copy(me, cols, turn, from_ref, to_ref, sems):
    step = (turn * (cols // 2 - 1)) % cols
    other = (me + step) % cols
    return pltpu.make_async_remote_copy(
        src_ref=from_ref.at[other],
        dst_ref=to_ref.at[me],
        send_sem=sems[0].at[step],
        recv_sem=sems[1].at[step],
        device_id={"col": other},
    )


def bulk_start(me, cols, lower, upper, from_ref, to_ref, sems):
    def send(step, carry):
        bulk_copy(me, cols, step, from_ref, to_ref, sems).start()
        return carry

    lax.fori_loop(lower, upper, send, 0)


def bulk_wait(me, cols, from_ref, to_ref, sems):
    def finish(step, carry):
        bulk_copy(me, cols, step, from_ref, to_ref, sems).wait()
        return carry

    lax.fori_loop(1, cols, finish, 0)


def groups_of(cols, levels):
    return [1 + (cols - 1) * i // levels for i in range(levels + 1)]


def early_groups(cols, levels):
    return [1] + [cols] * levels


def exchange_kernel(cols, from_ref, to_ref, *sems):
    me = lax.axis_index("col")
    greet(me, cols)
    bulk_start(me, cols, 1, cols, from_ref, to_ref, sems)
    to_ref[me] = from_ref[me]
    bulk_wait(me, cols, from_ref, to_ref, sems)


def direct_exchange(pieces, number):
    cols = pieces.shape[0]
    vmem = pl.BlockSpec(memory_space=pltpu.VMEM)
    return pl.pallas_call(
        functools.partial(exchange_kernel, cols),
        out_shape=jax.ShapeDtypeStruct(pieces.shape, pieces.dtype),
        in_specs=[vmem],
        out_specs=vmem,
        scratch_shapes=[pltpu.SemaphoreType.DMA((cols,))] * 2,
        compiler_params=pltpu.CompilerParams(collective_id=number, has_side_effects=True),
        cost_estimate=pl.CostEstimate(flops=3 * 10**10, bytes_accessed=4 * pieces.size, transcendentals=0),
        name="direct_exchange",
    )(pieces)


def gather_kernel(cols, levels, strip_ref, from_ref, all_ref, to_ref, send_sem, recv_sem, *sems):
    me = lax.axis_index("col")
    greet(me, cols)
    flags = [partner_of(me, levels - 1 - d)[0] for d in range(levels)]
    here = tuple(pl.ds(flag, 1) for flag in flags)
    bounds = groups_of(cols, levels)
    all_ref[here] = strip_ref[...].reshape((1,) * levels + strip_ref.shape)
    for dim in range(levels):
        region = (slice(None),) * dim + here[dim:]
        copy = pltpu.make_async_remote_copy(
            src_ref=all_ref.at[region],
            dst_ref=all_ref.at[region],
            send_sem=send_sem.at[dim],
            recv_sem=recv_sem.at[dim],
            device_id={"col": partner_of(me, levels - 1 - dim)[1]},
        )
        copy.start()
        bulk_start(me, cols, bounds[dim], bounds[dim + 1], from_ref, to_ref, sems)
        if dim == 0:
            to_ref[me] = from_ref[me]
        copy.wait()
    bulk_wait(me, cols, from_ref, to_ref, sems)


def gather_exchange(strip, pieces):
    cols = pieces.shape[0]
    levels = cols.bit_length() - 1
    vmem = pl.BlockSpec(memory_space=pltpu.VMEM)
    out, landed = pl.pallas_call(
        functools.partial(gather_kernel, cols, levels),
        out_shape=[
            jax.ShapeDtypeStruct((2,) * levels + strip.shape, strip.dtype),
            jax.ShapeDtypeStruct(pieces.shape, pieces.dtype),
        ],
        in_specs=[vmem, vmem],
        out_specs=[vmem, vmem],
        scratch_shapes=[pltpu.SemaphoreType.DMA((levels,))] * 2 + [pltpu.SemaphoreType.DMA((cols,))] * 2,
        compiler_params=pltpu.CompilerParams(collective_id=1, has_side_effects=True),
        cost_estimate=pl.CostEstimate(flops=3 * 10**10, bytes_accessed=4 * pieces.size, transcendentals=0),
        name="gather_exchange",
    )(strip, pieces)
    return out.reshape((cols,) + strip.shape), landed


def reduce_kernel(cols, levels, parts_ref, from_ref, sum_ref, to_ref, *scratch):
    landing, sums = scratch[:levels], scratch[levels : 2 * levels - 1]
    send_sem, recv_sem = scratch[2 * levels - 1 : 2 * levels + 1]
    sems = scratch[2 * levels + 1 :]
    me = lax.axis_index("col")
    greet(me, cols)
    bounds = early_groups(cols, levels)
    source = parts_ref
    for bit in range(levels):
        dim = levels - 1 - bit
        flag, partner = partner_of(me, bit)
        lead = (slice(None),) * dim
        tail = (slice(None),) * (bit + 2)
        copy = pltpu.make_async_remote_copy(
            src_ref=source.at[lead + (pl.ds(1 - flag, 1),) + tail],
            dst_ref=landing[bit],
            send_sem=send_sem.at[bit],
            recv_sem=recv_sem.at[bit],
            device_id={"col": partner},
        )
        copy.start()
        bulk_start(me, cols, bounds[bit], bounds[bit + 1], from_ref, to_ref, sems)
        if bit == 0:
            to_ref[me] = from_ref[me]
        copy.wait()
        mine = source[lead + (pl.ds(flag, 1),) + tail]
        total = mine.astype(jnp.float32) + landing[bit][...].astype(jnp.float32)
        if bit < levels - 1:
            source = sums[bit]
            source[...] = total.astype(source.dtype)
        else:
            sum_ref[...] = total.reshape(sum_ref.shape)
    bulk_wait(me, cols, from_ref, to_ref, sems)


def reduce_exchange(parts, pieces):
    cols, rows, width = parts.shape
    levels = cols.bit_length() - 1
    vmem = pl.BlockSpec(memory_space=pltpu.VMEM)
    shapes = [(2,) * (levels - 1 - bit) + (1,) * (bit + 1) + (rows, width) for bit in range(levels)]
    return pl.pallas_call(
        functools.partial(reduce_kernel, cols, levels),
        out_shape=[
            jax.ShapeDtypeStruct((rows, width), jnp.float32),
            jax.ShapeDtypeStruct(pieces.shape, pieces.dtype),
        ],
        in_specs=[vmem, vmem],
        out_specs=[vmem, vmem],
        scratch_shapes=[pltpu.VMEM(shape, parts.dtype if bit < 2 else jnp.float32) for bit, shape in enumerate(shapes)]
        + [pltpu.VMEM(shape, jnp.float32 if bit else parts.dtype) for bit, shape in enumerate(shapes[:-1])]
        + [pltpu.SemaphoreType.DMA((levels,))] * 2 + [pltpu.SemaphoreType.DMA((cols,))] * 2,
        compiler_params=pltpu.CompilerParams(collective_id=2, has_side_effects=True),
        cost_estimate=pl.CostEstimate(flops=3 * 10**10, bytes_accessed=4 * pieces.size, transcendentals=0),
        name="reduce_exchange",
    )(parts.reshape((2,) * levels + (rows, width)), pieces)


def body(queries, key_rows, value_rows, out_grad, dropout_bits, partner, block_pick, global_blocks):
    tokens_here, width = queries.shape
    blocks = tokens_here // BLOCK
    bands, cols = lax.axis_size("row"), lax.axis_size("col")
    band, place = lax.axis_index("row"), lax.axis_index("col")
    rows = BLOCK // cols
    part = width // CHUNKS
    size = bands * cols
    up = [(i, (i + 1) % size) for i in range(size)]
    down = [(j, i) for i, j in up]
    ordering = lax.dynamic_index_in_dim(partner, band, 1, keepdims=False)
    picks = lax.dynamic_index_in_dim(block_pick, band, 1, keepdims=False)
    col_ids = jnp.arange(cols, dtype=jnp.int32)
    hits = ordering[:, :, None] == col_ids[None, None, :]
    inverse = jnp.sum(jnp.where(hits, col_ids[None, :, None], 0), axis=1)
    asked = jnp.sum(jnp.where(hits, picks[:, :, None], 0), axis=1)
    wanted_ids = (ordering * blocks + picks).T.reshape(-1)
    band_start = band * cols * blocks
    global_ids = jnp.clip(global_blocks - band_start, 0, cols * blocks - 1)
    bits = dropout_bits.reshape(blocks, BLOCK, -1).swapaxes(1, 2)
    attended, query_grad, key_grad, value_grad = [], [], [], []
    for chunk in range(CHUNKS):
        lower, upper = chunk * part, (chunk + 1) * part
        both = jnp.concatenate([key_rows[:, lower:upper], value_rows[:, lower:upper]], 1)
        own_strips = both.reshape(blocks, cols, rows, 2 * part).swapaxes(0, 1)
        spread = direct_exchange(own_strips.reshape(cols, blocks * rows, 2 * part), 3)
        strips = spread.reshape(cols * blocks, rows, 2 * part)
        global_strips = jnp.take(strips, global_ids, axis=0)
        owners = global_blocks // (cols * blocks)
        chosen = global_strips
        for step in range(1, bands):
            ring = [(i, (i + step) % bands) for i in range(bands)]
            other = lax.ppermute(global_strips, "row", ring)
            chosen = jnp.where((owners == (band - step) % bands)[:, None, None], other, chosen)
        sent = jnp.take(strips, wanted_ids, axis=0).reshape(cols, NMATCH, rows, 2 * part)
        shared, fetched = gather_exchange(
            chosen.reshape(NGLOBAL * rows, 2 * part), sent.reshape(cols, NMATCH * rows, 2 * part)
        )
        shared = shared.reshape(cols, NGLOBAL, rows, 2 * part).swapaxes(0, 1).reshape(NGLOBAL * BLOCK, 2 * part)
        fetched = fetched.reshape(cols, NMATCH, rows, 2 * part)
        fetched = fetched.swapaxes(0, 1).reshape(NMATCH * BLOCK, 2 * part)
        before = lax.ppermute(both[tokens_here - BLOCK :], ("row", "col"), up)
        after = lax.ppermute(both[:BLOCK], ("row", "col"), down)
        att, qgrad, own, rims, far = attention(
            queries, out_grad, key_rows, value_rows, before, after, shared, fetched, bits, chunk
        )
        attended.append(att)
        query_grad.append(qgrad)
        from_next = lax.ppermute(rims[:, :BLOCK], ("row", "col"), down)
        from_last = lax.ppermute(rims[:, BLOCK:], ("row", "col"), up)
        slots = NGLOBAL + NMATCH
        pieces = far.reshape(2, slots, cols, rows, part).transpose(2, 1, 0, 3, 4)
        strips_sum, landed = reduce_exchange(
            pieces[:, :NGLOBAL].reshape(cols, NGLOBAL * 2 * rows, part),
            pieces[:, NGLOBAL:].reshape(cols, NMATCH * 2 * rows, part),
        )
        landed = landed.reshape(cols, NMATCH, 2, rows, part)
        band_sum = strips_sum.reshape(NGLOBAL, 2, rows, part)
        global_sum = band_sum
        for step in range(1, bands):
            ring = [(i, (i + step) % bands) for i in range(bands)]
            global_sum = global_sum + lax.ppermute(band_sum, "row", ring)
        block_ids = (band_start + jnp.arange(cols * blocks, dtype=jnp.int32)).reshape(cols, blocks)
        local_ids = jnp.arange(blocks, dtype=jnp.int32)
        returned = jnp.zeros((cols, blocks, 2, rows, part), jnp.float32)
        for matching in range(NMATCH):
            moved = jnp.take(landed[:, matching], inverse[matching], axis=0).astype(jnp.float32)
            mine = asked[matching][:, None] == local_ids[None, :]
            returned = returned + jnp.where(mine[:, :, None, None, None], moved[:, None], 0.0)
        for g in range(NGLOBAL):
            mine = block_ids == global_blocks[g]
            returned = returned + jnp.where(mine[:, :, None, None, None], global_sum[g][None, None], 0.0)
        home = direct_exchange(returned.astype(jnp.bfloat16).reshape(cols, blocks * 2 * rows, part), 4)
        home = home.reshape(cols, blocks, 2, rows, part).transpose(2, 1, 0, 3, 4).reshape(2, tokens_here, part)
        total = own + home.astype(jnp.float32)
        room = ((0, 0), (0, tokens_here - BLOCK), (0, 0))
        total = total + jnp.pad(from_last.astype(jnp.float32), room)
        total = total + jnp.pad(from_next.astype(jnp.float32), (room[0], room[1][::-1], room[2]))
        key_grad.append(total[0].astype(jnp.bfloat16))
        value_grad.append(total[1].astype(jnp.bfloat16))
    return tuple(jnp.concatenate(parts, 1) for parts in (attended, query_grad, key_grad, value_grad))


def solution(mesh):
    split = P(("row", "col"), None)
    return jax.shard_map(
        body,
        mesh=mesh,
        in_specs=(split,) * 5 + (P(),) * 3,
        out_specs=(split,) * 4,
        check_vma=False,
    )
```

profile of v0, /device:TPU:1, one launch (start us, length us, event | category | flops | bytes accessed | tf_op | source)
XLA Modules:
  0.0 222.3 jit_solution(13883228173911205541)
XLA Ops:
  0.6 0.0 copy-start
  0.7 0.7 copy-done
  1.3 0.7 constant_dynamic-slice_fusion.1
  2.0 0.1 select_reduce_fusion.1
  2.1 1.1 constant_dynamic-update-slice_fusion.1
  3.2 1.1 constant_dynamic-update-slice_fusion
  4.3 1.0 copy.58
  5.4 31.9 %direct_exchange.2 = bf16[16,16,2048]{2,1,0:T(8,128)(2,1)} custom-call(bf16[16,16,2048]{2,1,0:T(8,128)(2,1)} %bitcast.136), custom_call_target="tpu_custom_call" | custom-call | flops 30000001024 | bytes 2097152 | tf_op jit(solution)/shard_map/direct_exchange/pallas_call | solution.py:225
  37.2 0.0 copy-start.1
  37.3 0.0 copy-done.7
  37.3 1.9 gather_fusion
  39.2 0.1 broadcast_select_fusion
  39.2 1.2 collective-permute-start.2
  40.5 0.9 fusion.13
  41.4 1.9 collective-permute-start
  43.3 0.0 collective-permute-start.1
  43.3 0.6 fusion.14
  43.9 0.1 copy.34
  44.0 0.1 reshape.215
  44.1 0.7 gather_fusion.1
  44.8 0.1 copy.33
  44.9 0.0 copy-done.6
  44.9 0.8 copy.37
  45.7 0.1 copy.40
  45.8 0.1 copy.41
  45.9 0.1 copy.38
  46.0 1.3 fusion.8
  47.3 0.1 copy.42
  47.4 0.1 copy.43
  47.5 1.4 bitcast_select_fusion.3.from_ref
  48.8 0.0 collective-permute-done.2
  48.8 0.7 select_bitcast_fusion.strip_ref
  49.5 44.8 %gather_exchange.1 = (bf16[2,2,2,2,16,2048]{5,4,3,2,1,0:T(8,128)(2,1)}, bf16[16,24,2048]{2,1,0:T(8,128)(2,1)}) custom-call(bf16[16,2048]{1,0:T(8,128)(2,1)} %select_bitcast_fusion.strip_ref, bf16[16,24,2048]{2,1,0:T(8,128)(2,1)} %bitcast_select_fusion.3.from_ref), custom_call_target="tpu_custom_call" | custom-call | flops 30000001024 | bytes 3145728 | tf_op jit(solution)/shard_map/gather_exchange/pallas_call | solution.py:265
  94.3 0.0 copy-start.4
  94.3 2.9 %copy.36 = bf16[16,3,8,2048]{3,2,0,1:T(8,128)(2,1)} copy(bf16[16,3,8,2048]{3,2,1,0:T(8,128)(2,1)} %bitcast.129) | data formatting | bytes 3145728 | tf_op jit(solution)/shard_map/reshape | solution.py:377
  97.2 1.1 copy.35
  98.4 0.0 collective-permute-done.kp_ref.vp_ref
  98.4 0.0 collective-permute-done.1.kn_ref.vn_ref
  98.4 24.5 %block_attention.1 = (bf16[256,1024]{1,0:T(8,128)(2,1)}, bf16[256,1024]{1,0:T(8,128)(2,1)}, f32[2,256,1024]{2,1,0:T(8,128)}, bf16[2,256,1024]{2,1,0:T(8,128)(2,1)}, bf16[2,640,1024]{2,1,0:T(8,128)(2,1)}) custom-call(bf16[256,1024]{1,0:T(8,128)(2,1)} %q_ref.1, bf16[256,1024]{1,0:T(8,128)(2,1)} %g_ref.1, bf16[256,1024]{1,0:T(8,128)(2,1)} %ko_ref.1, ...), custom_call_target="tpu_custom_call" | custom-call | flops 3758096384 | bytes 4194304 | tf_op jit(solution)/shard_map/block_attention/pallas_call | solution.py:136
  122.9 2.0 copy.57
  124.9 1.3 slice.99
  126.3 1.1 slice.98
  127.3 46.8 %reduce_exchange.1 = (f32[32,1024]{1,0:T(8,128)}, bf16[16,48,1024]{2,1,0:T(8,128)(2,1)}) custom-call(bf16[2,2,2,2,32,1024]{5,4,3,2,1,0:T(8,128)(2,1)} %bitcast.135, bf16[16,48,1024]{2,1,0:T(8,128)(2,1)} %bitcast.130), custom_call_target="tpu_custom_call" | custom-call | flops 30000001024 | bytes 3145728 | tf_op jit(solution)/shard_map/reduce_exchange/pallas_call | solution.py:321
  174.2 1.6 slice_bitcast_fusion.4
  175.8 0.6 collective-permute-start.3
  176.4 1.1 fusion.12
  177.5 1.4 collective-permute-start.4
  178.9 0.0 collective-permute-start.5
  178.9 0.6 gather_fusion.2
  179.5 0.1 select_convert_fusion.2
  179.6 0.6 gather_fusion.4
  180.2 0.1 select_convert_fusion
  180.3 0.6 gather_fusion.3
  180.9 0.1 select_convert_fusion.1
  181.1 0.0 collective-permute-done.3
  181.2 1.8 fusion.6.from_ref
  183.0 33.4 %direct_exchange.3 = bf16[16,32,1024]{2,1,0:T(8,128)(2,1)} custom-call(bf16[16,32,1024]{2,1,0:T(8,128)(2,1)} %fusion.6.from_ref), custom_call_target="tpu_custom_call" | custom-call | flops 30000001024 | bytes 2097152 | tf_op jit(solution)/shard_map/direct_exchange/pallas_call | solution.py:225
  216.3 1.5 convert_bitcast_fusion
  217.8 0.1 copy.44
  218.0 0.0 collective-permute-done.4
  218.0 0.0 collective-permute-done.5
  218.0 1.4 copy-done.2
  219.4 1.8 fusion.2
  221.2 1.0 slice_bitcast_fusion
  (32 shorter events, 0.2 us)
Async XLA Ops:
  0.6 0.7 copy-start
  5.4 31.9 %copy-start.7 = (s32[2]{0:T(128)S(1)}, s32[2]{0:T(128)}, u32[]{:S(2)}) copy-start(s32[2]{0:T(128)} %param.17) | copy-start | bytes 28
  37.2 6.9 %copy-start.1 = (bf16[16,16,2048]{2,1,0:T(8,128)(2,1)S(1)}, bf16[16,16,2048]{2,1,0:T(8,128)(2,1)}, u32[]{:S(2)}) copy-start(bf16[16,16,2048]{2,1,0:T(8,128)(2,1)} %direct_exchange.2) | copy-start | bytes 3145732
  39.2 9.6 %collective-permute-start.2 = (bf16[2,8,2048]{2,1,0:T(8,128)(2,1)S(1)}, bf16[2,8,2048]{2,1,0:T(8,128)(2,1)S(1)}, u32[]{:S(2)}, u32[]{:S(2)}) collective-permute-start(bf16[2,8,2048]{2,1,0:T(8,128)(2,1)S(1)} %broadcast_select_fusion), channel_id=1, source_target_pairs={{0,16},{16,0},{1,17},{17,1},{2,18},{18,2},{3,19},{19,3},{4,20},{20... | collective-permute-start | bytes 196616 | tf_op jit(solution)/shard_map/ppermute | solution.py:370
  41.4 3.5 %copy-start.6 = (s32[256,128]{1,0:T(8,128)S(1)}, s32[256,128]{1,0:T(8,128)}, u32[]{:S(2)}) copy-start(s32[256,128]{1,0:T(8,128)} %param.14) | copy-start | bytes 393220
  41.4 57.0 %collective-permute-start = (bf16[128,2048]{1,0:T(8,128)(2,1)}, bf16[128,2048]{1,0:T(8,128)(2,1)}, u32[]{:S(2)}, u32[]{:S(2)}) collective-permute-start(bf16[128,2048]{1,0:T(8,128)(2,1)} %get-tuple-element.43), channel_id=1, source_target_pairs={{0,1},{1,2},{2,3},{3,4},{4,5},{5,6},{6,7},{7,8},{8,9},{9,10},{10,1... | collective-permute-start | bytes 1572872 | tf_op jit(solution)/shard_map/ppermute | solution.py:379
  43.3 55.0 %collective-permute-start.1 = (bf16[128,2048]{1,0:T(8,128)(2,1)S(1)}, bf16[128,2048]{1,0:T(8,128)(2,1)}, u32[]{:S(2)}, u32[]{:S(2)}) collective-permute-start(bf16[128,2048]{1,0:T(8,128)(2,1)S(1)} %get-tuple-element.42), channel_id=1, source_target_pairs={{1,0},{2,1},{3,2},{4,3},{5,4},{6,5},{7,6},{8,7},{9,8},{10,9},{11,1... | collective-permute-start | bytes 1572872 | tf_op jit(solution)/shard_map/ppermute | solution.py:380
  94.3 2.9 %copy-start.4 = (bf16[2,2,2,2,16,2048]{5,4,3,2,1,0:T(8,128)(2,1)S(1)}, bf16[2,2,2,2,16,2048]{5,4,3,2,1,0:T(8,128)(2,1)}, u32[]{:S(2)}) copy-start(bf16[2,2,2,2,16,2048]{5,4,3,2,1,0:T(8,128)(2,1)} %get-tuple-element.14) | copy-start | bytes 3145732
  174.2 1.6 copy-start.5
  174.2 2.2 %copy-start.3 = (bf16[2,256,1024]{2,1,0:T(8,128)(2,1)S(1)}, bf16[2,256,1024]{2,1,0:T(8,128)(2,1)}, u32[]{:S(2)}) copy-start(bf16[2,256,1024]{2,1,0:T(8,128)(2,1)} %get-tuple-element.22) | copy-start | bytes 3145732
  175.8 5.2 %collective-permute-start.3 = (f32[2,2,8,1024]{3,2,1,0:T(8,128)S(1)}, f32[2,2,8,1024]{3,2,1,0:T(8,128)S(1)}, u32[]{:S(2)}, u32[]{:S(2)}) collective-permute-start(f32[2,2,8,1024]{3,2,1,0:T(8,128)S(1)} %bitcast.139), channel_id=1, source_target_pairs={{0,16},{16,0},{1,17},{17,1},{2,18},{18,2},{3,19},{19,3},{4,20},{20... | collective-permute-start | bytes 393224 | tf_op jit(solution)/shard_map/ppermute | solution.py:399
  177.5 40.5 %collective-permute-start.4 = (bf16[2,128,1024]{2,1,0:T(8,128)(2,1)}, bf16[2,128,1024]{2,1,0:T(8,128)(2,1)}, u32[]{:S(2)}, u32[]{:S(2)}) collective-permute-start(bf16[2,128,1024]{2,1,0:T(8,128)(2,1)} %get-tuple-element.40), channel_id=1, source_target_pairs={{0,1},{1,2},{2,3},{3,4},{4,5},{5,6},{6,7},{7,8},{8,9},{9,10},{10,1... | collective-permute-start | bytes 1572872 | tf_op jit(solution)/shard_map/ppermute | solution.py:387
  178.9 39.1 %collective-permute-start.5 = (bf16[2,128,1024]{2,1,0:T(8,128)(2,1)}, bf16[2,128,1024]{2,1,0:T(8,128)(2,1)}, u32[]{:S(2)}, u32[]{:S(2)}) collective-permute-start(bf16[2,128,1024]{2,1,0:T(8,128)(2,1)} %get-tuple-element.41), channel_id=1, source_target_pairs={{1,0},{2,1},{3,2},{4,3},{5,4},{6,5},{7,6},{8,7},{9,8},{10,9},{11,1... | collective-permute-start | bytes 1572872 | tf_op jit(solution)/shard_map/ppermute | solution.py:386
  217.8 1.6 copy-start.2
where the time goes:
time: 223 us; the launch traced here: 222 us
  Pallas kernels  181 us (81%)
  local copies, waits for them, and re-layouts  25.5 us (11%)
  other arithmetic  9.16 us (4%)
  starting transfers between devices  5.14 us (2%)
    pallas_call x2, Pallas kernels, direct_exchange(): pl.pallas_call(functools.partial(exchange_kernel, cols), out_shape=jax.Sh...  65.2 us
    pallas_call x1, Pallas kernels, reduce_exchange(): pl.pallas_call(functools.partial(reduce_kernel, cols, levels), out_shape=...  46.8 us
    pallas_call x1, Pallas kernels, gather_exchange(): pl.pallas_call(functools.partial(gather_kernel, cols, levels), out_shape=...  44.8 us
    pallas_call x1, Pallas kernels, attention(): pl.pallas_call(functools.partial(attention_kernel, blocks), grid=(pairs,)...  24.5 us
  transfers between devices with their start and end apart: 6, of which 0 were waited for; matrix products, arithmetic and copies ran while one was open for 8% of the time, Pallas kernels for 35%

commit v1 on v0

v1 whole, which is shorter than its diff:
```python
import functools

import jax
import jax.numpy as jnp
from jax import lax
from jax.experimental import pallas as pl
from jax.experimental.pallas import tpu as pltpu
from jax.sharding import PartitionSpec as P

HEAD_DIM = 64
BLOCK = 128
NGLOBAL = 2
NMATCH = 3
PAIR = 2 * HEAD_DIM
SLOTS = 3 + NGLOBAL + NMATCH

score_scale = 0.125
keep_scale = 1.0 / 0.9


def contract(a, b, dim_a, dim_b):
    return lax.dot_general(a, b, (((dim_a,), (dim_b,)), ((), ())), preferred_element_type=jnp.float32)


def stride_of(count):
    return max(1, count // 2 - 1)


def fused_kernel(
    rows, cols, heads, blocks,
    q_ref, k_ref, v_ref, g_ref, bits_ref, partner_ref, pick_ref, global_ref,
    qa_land, kvg_land,
    kv_pack, qg_pack, kv_in, qg_in, bits_all, kv_ext, kv_turned, halo, shared, shared_turned,
    shared_keys, words_ref, s_ref, dsp_ref, acc_ref, rand_ref, gacc_ref, halo_acc, gacc_in, qa_out, kvg_out, inverse_ref,
    kv_send, kv_recv, qg_send, qg_recv, bit_send, bit_recv, row_send, row_recv, back_send, back_recv, qa_send, qa_recv, kvg_send, kvg_recv,
):
    me, band = lax.axis_index("col"), lax.axis_index("row")
    head, group = me % heads, me // heads
    levels = heads.bit_length() - 1
    last = cols * blocks
    first = lax.broadcasted_iota(jnp.int32, (BLOCK, PAIR), 1) < HEAD_DIM
    zero = jnp.zeros((BLOCK, PAIR), jnp.bfloat16)

    barrier = pltpu.get_barrier_semaphore()

    def hello(step, carry):
        pl.semaphore_signal(barrier, inc=1, device_id={"col": (me + step) % cols})
        return carry

    lax.fori_loop(1, cols, hello, 0)
    for step in range(1, rows):
        pl.semaphore_signal(barrier, inc=1, device_id={"row": (band + step) % rows})

    for p in range(heads // 2):
        lanes = slice(p * PAIR, (p + 1) * PAIR)
        keys, values = k_ref[:, lanes], v_ref[:, lanes]
        left = jnp.concatenate([keys[:, :HEAD_DIM], values[:, :HEAD_DIM]], axis=1)
        right = jnp.concatenate([keys[:, HEAD_DIM:], values[:, HEAD_DIM:]], axis=1)
        kv_pack[2 * p] = left.reshape(blocks, BLOCK, PAIR)
        kv_pack[2 * p + 1] = right.reshape(blocks, BLOCK, PAIR)
    flags = [(me // 2 ** (levels - 1 - d)) % 2 for d in range(levels)]
    here = tuple(pl.ds(flag, 1) for flag in flags)
    for j in range(blocks):
        words = bits_ref[j * BLOCK : (j + 1) * BLOCK, :].astype(jnp.float32).T.astype(jnp.bfloat16)
        bits_all[here + (j,)] = words.reshape((1,) * levels + words.shape)

    pl.semaphore_wait(barrier, cols - 1 + rows - 1)

    def kv_copy(turn):
        step = (turn * stride_of(cols)) % cols
        other = (me + step) % cols
        return pltpu.make_async_remote_copy(
            src_ref=kv_pack.at[other % heads],
            dst_ref=kv_in.at[turn],
            send_sem=kv_send.at[step],
            recv_sem=kv_recv.at[step],
            device_id={"col": other},
        )

    def kv_start(turn, carry):
        kv_copy(turn).start()
        return carry

    bounds = [1 + (cols - 1) * i // levels for i in range(levels + 1)]

    def bits_copy(dim):
        bit = levels - 1 - dim
        region = (slice(None),) * dim + here[dim:]
        return pltpu.make_async_remote_copy(
            src_ref=bits_all.at[region],
            dst_ref=bits_all.at[region],
            send_sem=bit_send.at[dim],
            recv_sem=bit_recv.at[dim],
            device_id={"col": me + 2**bit - 2 * 2**bit * flags[dim]},
        )

    for dim in range(levels):
        copy = bits_copy(dim)
        copy.start()
        lax.fori_loop(bounds[dim], bounds[dim + 1], kv_start, 0)
        if dim == 0:
            for p in range(heads // 2):
                lanes = slice(p * PAIR, (p + 1) * PAIR)
                query = (q_ref[:, lanes].astype(jnp.float32) * score_scale).astype(jnp.bfloat16)
                grad = g_ref[:, lanes]
                qg_pack[2 * p] = jnp.concatenate([query[:, :HEAD_DIM], grad[:, :HEAD_DIM]], axis=1)
                qg_pack[2 * p + 1] = jnp.concatenate([query[:, HEAD_DIM:], grad[:, HEAD_DIM:]], axis=1)
        copy.wait()

    def qg_copy(turn):
        step = (turn * stride_of(heads)) % heads
        other = (head + step) % heads
        return pltpu.make_async_remote_copy(
            src_ref=qg_pack.at[other],
            dst_ref=qg_in.at[turn],
            send_sem=qg_send.at[step],
            recv_sem=qg_recv.at[step],
            device_id={"col": group * heads + other},
        )

    def qg_start(turn, carry):
        qg_copy(turn).start()
        return carry

    lax.fori_loop(1, heads, qg_start, 0)
    qg_in[0] = qg_pack[head]

    def find(place, carry):
        for r in range(NMATCH):
            def look(c, found):
                return found + jnp.where(partner_ref[r, band, c] == place, c, 0)

            inverse_ref[r, place] = jnp.minimum(lax.fori_loop(0, cols, look, 0), cols - 1)
        return carry

    lax.fori_loop(0, cols, find, 0)

    def clear(i, carry):
        acc_ref[i] = jnp.zeros((BLOCK, PAIR), jnp.float32)
        return carry

    lax.fori_loop(0, last + 2, clear, 0)
    gacc_ref[...] = jnp.zeros_like(gacc_ref)

    def turn_block(value):
        return value.astype(jnp.float32).T.astype(jnp.bfloat16)

    def place_kv(turn):
        source = (me + turn * (cols - stride_of(cols))) % cols
        for j in range(blocks):
            value = kv_in[turn, j]
            kv_ext[1 + source * blocks + j] = value
            kv_turned[1 + source * blocks + j] = turn_block(value)

    kv_in[0] = kv_pack[head]
    place_kv(0)

    def kv_take(turn, carry):
        kv_copy(turn).wait()
        place_kv(turn)
        return carry

    lax.fori_loop(1, cols, kv_take, 0)

    def edge_copies():
        return [
            pltpu.make_async_remote_copy(
                src_ref=kv_ext.at[last],
                dst_ref=halo.at[0],
                send_sem=row_send.at[0],
                recv_sem=row_recv.at[0],
                device_id={"row": (band + 1) % rows},
            ),
            pltpu.make_async_remote_copy(
                src_ref=kv_ext.at[1],
                dst_ref=halo.at[1],
                send_sem=row_send.at[1],
                recv_sem=row_recv.at[1],
                device_id={"row": (band + rows - 1) % rows},
            ),
        ]

    def shared_copy(step):
        return pltpu.make_async_remote_copy(
            src_ref=shared.at[band],
            dst_ref=shared.at[band],
            send_sem=row_send.at[1 + step],
            recv_sem=row_recv.at[1 + step],
            device_id={"row": (band + step) % rows},
        )

    for n in range(NGLOBAL):
        shared[band, n] = kv_ext[1 + jnp.clip(global_ref[n] - band * last, 0, last - 1)]
    for copy in edge_copies():
        copy.start()
    for step in range(1, rows):
        shared_copy(step).start()
    for copy in edge_copies():
        copy.wait()
    for side, place in ((0, 0), (1, last + 1)):
        value = halo[side]
        kv_ext[place] = value
        kv_turned[place] = turn_block(value)
    for step in range(1, rows):
        shared_copy(step).wait()
    for n in range(NGLOBAL):
        value = shared[global_ref[n] // last, n]
        shared_keys[n] = value
        shared_turned[n] = turn_block(value)

    for slot in range(heads):
        where_bits = tuple((slot // 2 ** (levels - 1 - d)) % 2 for d in range(levels))
        words_ref[slot] = bits_all[where_bits].astype(jnp.float32).astype(jnp.int32)

    wide = 2 * BLOCK
    marks = jnp.left_shift(1, lax.broadcasted_iota(jnp.int32, (BLOCK // 8, 8, BLOCK), 1))

    def attend(turn):
        slot = (head + turn * (heads - stride_of(heads))) % heads
        place = group * heads + slot
        far = [1 + partner_ref[r, band, place] * blocks + pick_ref[r, band, place] for r in range(NMATCH)]
        far_keys = [shared_keys[n] for n in range(NGLOBAL)] + [kv_ext[b] for b in far]
        near_keys = [kv_ext[place * blocks + b] for b in range(blocks + 2)]
        sides = []
        for j in range(blocks):
            packed = qg_in[turn, j * BLOCK : (j + 1) * BLOCK, :]
            side = jnp.concatenate([jnp.where(first, packed, zero), jnp.where(first, zero, packed)], axis=0)
            sides.append(side)
            keys = near_keys[j : j + 3] + far_keys
            top = None
            for i in range(SLOTS):
                both = contract(keys[i], side, 1, 1)
                s_ref[i] = both
                part = jnp.max(both[:, :BLOCK].reshape(BLOCK // 8, 8, BLOCK), axis=0)
                top = part if top is None else jnp.maximum(top, part)
            top = jnp.max(top, axis=0, keepdims=True)
            total, mixed = None, None
            for i in range(SLOTS):
                words = words_ref[slot, j, i * BLOCK // 8 : (i + 1) * BLOCK // 8, :]
                keep = (jnp.broadcast_to(words[:, None, :], marks.shape) & marks) != 0
                weight = jnp.exp(s_ref[i, :, :BLOCK] - top).reshape(marks.shape)
                grad_p = jnp.where(keep, s_ref[i, :, BLOCK:].reshape(marks.shape), 0.0)
                s_ref[i, :, :BLOCK] = weight.reshape(BLOCK, BLOCK)
                s_ref[i, :, BLOCK:] = grad_p.reshape(BLOCK, BLOCK)
                part = jnp.sum(weight, axis=0)
                cross = jnp.sum(weight * grad_p, axis=0)
                total = part if total is None else total + part
                mixed = cross if mixed is None else mixed + cross
            inverse = 1.0 / jnp.sum(total, axis=0, keepdims=True)
            delta = jnp.sum(mixed, axis=0, keepdims=True) * inverse
            scaled = inverse * keep_scale
            for i in range(SLOTS):
                words = words_ref[slot, j, i * BLOCK // 8 : (i + 1) * BLOCK // 8, :]
                keep = (jnp.broadcast_to(words[:, None, :], marks.shape) & marks) != 0
                probs = s_ref[i, :, :BLOCK] * scaled
                dscore = probs * (s_ref[i, :, BLOCK:] - delta)
                dropped = jnp.where(keep, probs.reshape(marks.shape), 0.0).reshape(BLOCK, BLOCK)
                dsp_ref[j, i, :, :BLOCK] = dscore.astype(jnp.bfloat16)
                dsp_ref[j, i, :, BLOCK:] = dropped.astype(jnp.bfloat16)
            turned = [kv_turned[place * blocks + j + b] for b in range(3)]
            turned += [shared_turned[n] for n in range(NGLOBAL)] + [kv_turned[b] for b in far]
            out = contract(jnp.concatenate(turned, axis=1), dsp_ref[j].reshape(SLOTS * BLOCK, wide), 1, 0)
            out = jnp.concatenate([out[:HEAD_DIM, :BLOCK] * score_scale, out[HEAD_DIM:, BLOCK:]], axis=0)
            qa_out[turn, j * BLOCK : (j + 1) * BLOCK, :] = out.T.astype(jnp.bfloat16)
        for j in range(blocks):
            grads = contract(dsp_ref[j, :3].reshape(3 * BLOCK, wide), sides[j], 1, 0)
            for b in range(3):
                acc_ref[place * blocks + j + b] += grads[b * BLOCK : (b + 1) * BLOCK]
        grads = None
        for j in range(blocks):
            part = contract(dsp_ref[j, 3:].reshape((SLOTS - 3) * BLOCK, wide), sides[j], 1, 0)
            grads = part if grads is None else grads + part
        for n in range(NGLOBAL):
            gacc_ref[n] += grads[n * BLOCK : (n + 1) * BLOCK]
        for r in range(NMATCH):
            rand_ref[slot, r] = grads[(NGLOBAL + r) * BLOCK : (NGLOBAL + r + 1) * BLOCK]

    def qa_copy(turn):
        step = (turn * stride_of(heads)) % heads
        slot = (head - step + heads) % heads
        return pltpu.make_async_remote_copy(
            src_ref=qa_out.at[turn],
            dst_ref=qa_land.at[head],
            send_sem=qa_send.at[step],
            recv_sem=qa_recv.at[step],
            device_id={"col": group * heads + slot},
        )

    def segment(turn, carry):
        qg_copy(turn).wait()
        attend(turn)
        qa_copy(turn).start()
        return carry

    attend(0)
    lax.fori_loop(1, heads, segment, 0)
    qa_land[head] = qa_out[0]

    def back_copies():
        copies = [
            pltpu.make_async_remote_copy(
                src_ref=acc_ref.at[last + 1],
                dst_ref=halo_acc.at[0],
                send_sem=back_send.at[0],
                recv_sem=back_recv.at[0],
                device_id={"row": (band + 1) % rows},
            ),
            pltpu.make_async_remote_copy(
                src_ref=acc_ref.at[0],
                dst_ref=halo_acc.at[1],
                send_sem=back_send.at[1],
                recv_sem=back_recv.at[1],
                device_id={"row": (band + rows - 1) % rows},
            ),
        ]
        for step in range(1, rows):
            copies.append(
                pltpu.make_async_remote_copy(
                    src_ref=gacc_ref,
                    dst_ref=gacc_in.at[band],
                    send_sem=back_send.at[1 + step],
                    recv_sem=back_recv.at[1 + step],
                    device_id={"row": (band + step) % rows},
                )
            )
        return copies

    for copy in back_copies():
        copy.start()
    for copy in back_copies():
        copy.wait()
    sums = []
    for n in range(NGLOBAL):
        total = gacc_ref[n]
        for step in range(1, rows):
            total = total + gacc_in[(band + step) % rows, n]
        s_ref[n, :, :BLOCK] = total
    acc_ref[1] += halo_acc[0]
    acc_ref[last] += halo_acc[1]

    def collect(turn):
        place = (me + turn * stride_of(cols)) % cols
        totals = [acc_ref[1 + place * blocks + j] for j in range(blocks)]
        for r in range(NMATCH):
            source = inverse_ref[r, place]
            chosen = jnp.where(source // heads == group, pick_ref[r, band, source], blocks)
            part = rand_ref[source % heads, r]
            totals = [total + jnp.where(chosen == j, part, 0.0) for j, total in enumerate(totals)]
        for n in range(NGLOBAL):
            chosen = global_ref[n] - (band * cols + place) * blocks
            part = s_ref[n, :, :BLOCK]
            totals = [total + jnp.where(chosen == j, part, 0.0) for j, total in enumerate(totals)]
        for j in range(blocks):
            kvg_out[turn, j] = totals[j].astype(jnp.bfloat16)

    def kvg_copy(turn):
        step = (turn * stride_of(cols)) % cols
        other = (me + step) % cols
        return pltpu.make_async_remote_copy(
            src_ref=kvg_out.at[turn],
            dst_ref=kvg_land.at[me],
            send_sem=kvg_send.at[step],
            recv_sem=kvg_recv.at[step],
            device_id={"col": other},
        )

    def give(turn, carry):
        collect(turn)
        kvg_copy(turn).start()
        return carry

    lax.fori_loop(1, cols, give, 0)
    collect(0)
    kvg_land[me] = kvg_out[0]

    def qa_finish(turn, carry):
        qa_copy(turn).wait()
        return carry

    lax.fori_loop(1, heads, qa_finish, 0)

    def kvg_finish(turn, carry):
        kvg_copy(turn).wait()
        return carry

    lax.fori_loop(1, cols, kvg_finish, 0)


def fused(rows, cols, queries, key_rows, value_rows, out_grad, bits, partner, pick, shared_ids):
    tokens_here, width = queries.shape
    blocks = tokens_here // BLOCK
    heads = width // HEAD_DIM
    levels = heads.bit_length() - 1
    last = cols * blocks
    half, full = jnp.bfloat16, jnp.float32
    vmem = pl.BlockSpec(memory_space=pltpu.VMEM)
    smem = pl.BlockSpec(memory_space=pltpu.SMEM)

    scratch = [
        pltpu.VMEM((heads, blocks, BLOCK, PAIR), half),
        pltpu.VMEM((heads, tokens_here, PAIR), half),
        pltpu.VMEM((cols, blocks, BLOCK, PAIR), half),
        pltpu.VMEM((heads, tokens_here, PAIR), half),
        pltpu.VMEM((2,) * levels + (blocks, BLOCK, BLOCK), half),
        pltpu.VMEM((last + 2, BLOCK, PAIR), half),
        pltpu.VMEM((last + 2, PAIR, BLOCK), half),
        pltpu.VMEM((2, BLOCK, PAIR), half),
        pltpu.VMEM((rows, NGLOBAL, BLOCK, PAIR), half),
        pltpu.VMEM((NGLOBAL, PAIR, BLOCK), half),
        pltpu.VMEM((NGLOBAL, BLOCK, PAIR), half),
        pltpu.VMEM((heads, blocks, BLOCK, BLOCK), jnp.int32),
        pltpu.VMEM((SLOTS, BLOCK, 2 * BLOCK), full),
        pltpu.VMEM((blocks, SLOTS, BLOCK, 2 * BLOCK), half),
        pltpu.VMEM((last + 2, BLOCK, PAIR), full),
        pltpu.VMEM((heads, NMATCH, BLOCK, PAIR), full),
        pltpu.VMEM((NGLOBAL, BLOCK, PAIR), full),
        pltpu.VMEM((2, BLOCK, PAIR), full),
        pltpu.VMEM((rows, NGLOBAL, BLOCK, PAIR), full),
        pltpu.VMEM((heads, tokens_here, PAIR), half),
        pltpu.VMEM((cols, blocks, BLOCK, PAIR), half),
        pltpu.SMEM((NMATCH, cols), jnp.int32),
    ]
    for count in (cols, heads, levels, rows + 1, rows + 1, heads, cols):
        scratch += [pltpu.SemaphoreType.DMA((count,))] * 2
    return pl.pallas_call(
        functools.partial(fused_kernel, rows, cols, heads, blocks),
        out_shape=[
            jax.ShapeDtypeStruct((heads, tokens_here, PAIR), half),
            jax.ShapeDtypeStruct((cols, blocks, BLOCK, PAIR), half),
        ],
        in_specs=[vmem] * 5 + [smem] * 3,
        out_specs=[vmem, vmem],
        scratch_shapes=scratch,
        compiler_params=pltpu.CompilerParams(collective_id=1, has_side_effects=True),
        name="head_attention",
    )(queries, key_rows, value_rows, out_grad, bits, partner, pick, shared_ids)


def unpack_kernel(groups, qa_ref, kvg_ref, att_ref, qg_ref, kg_ref, vg_ref):
    def split(pairs):
        left, right = pairs
        low = jnp.concatenate([left[:, :HEAD_DIM], right[:, :HEAD_DIM]], axis=1)
        high = jnp.concatenate([left[:, HEAD_DIM:], right[:, HEAD_DIM:]], axis=1)
        return low, high

    qg_ref[...], att_ref[...] = split([qa_ref[0], qa_ref[1]])
    totals = []
    for side in range(2):
        total = kvg_ref[0, side]
        if groups > 1:
            total = total.astype(jnp.float32)
            for g in range(1, groups):
                total = total + kvg_ref[g, side].astype(jnp.float32)
            total = total.astype(jnp.bfloat16)
        totals.append(total)
    kg_ref[...], vg_ref[...] = split(totals)


def unpack(qa, kvg):
    heads, tokens_here, _ = qa.shape
    groups = kvg.shape[0] // heads
    kvg = kvg.reshape(groups, heads, tokens_here, PAIR)
    flat = pl.BlockSpec((tokens_here, PAIR), lambda p: (0, p))
    shape = jax.ShapeDtypeStruct((tokens_here, heads * HEAD_DIM), jnp.bfloat16)
    return pl.pallas_call(
        functools.partial(unpack_kernel, groups),
        grid=(heads // 2,),
        in_specs=[
            pl.BlockSpec((2, tokens_here, PAIR), lambda p: (p, 0, 0)),
            pl.BlockSpec((groups, 2, tokens_here, PAIR), lambda p: (0, p, 0, 0)),
        ],
        out_specs=[flat] * 4,
        out_shape=[shape] * 4,
        name="unpack_heads",
    )(qa, kvg)


def body(queries, key_rows, value_rows, out_grad, dropout_bits, partner, block_pick, global_blocks):
    rows, cols = lax.axis_size("row"), lax.axis_size("col")
    qa, kvg = fused(
        rows, cols, queries, key_rows, value_rows, out_grad, dropout_bits, partner, block_pick, global_blocks
    )
    attended, query_grad, key_grad, value_grad = unpack(qa, kvg)
    return attended, query_grad, key_grad, value_grad


def solution(mesh):
    split = P(("row", "col"), None)
    return jax.shard_map(
        body,
        mesh=mesh,
        in_specs=(split,) * 5 + (P(),) * 3,
        out_specs=(split,) * 4,
        check_vma=False,
    )
```

time: 223 us -> 117 us (0.52)
  Pallas kernels: 181 us -> 116 us
  local copies, waits for them, and re-layouts: 25.5 us -> 0 us
  other arithmetic: 9.16 us -> 0 us
  starting transfers between devices: 5.14 us -> 0 us
    pallas_call x5 -> x2, Pallas kernels: 181 us -> 116 us  [the longest x1 110 us: fused(): pl.pallas_call(functools.partial(fused_kernel, rows, cols, heads, blocks)...]
    reshape x4 -> x0, local copies, waits for them, and re-layouts: 5.74 us -> none  [the longest x1 2.88 us: body(): fetched = fetched.reshape(cols, NMATCH, rows, 2 * part)]
    ppermute x6 -> x0, starting transfers between devices: 5.14 us -> none  [the longest x1 1.93 us: body(): before = lax.ppermute(both[tokens_here - BLOCK:], ('row', 'col'), up)]
    slice x5 -> x0, local copies, waits for them, and re-layouts: 4.93 us -> none  [the longest x1 1.32 us: body(): pieces[:, NGLOBAL:].reshape(cols, NMATCH * 2 * rows, part)]
    gather x5 -> x0, local copies, waits for them, and re-layouts: 4.25 us -> none  [the longest x1 1.85 us: body(): global_strips = jnp.take(strips, global_ids, axis=0)]
    convert_element_type x5 -> x0, other arithmetic: 3.68 us -> none  [the longest x1 1.79 us: body(): returned.astype(jnp.bfloat16).reshape(cols, blocks * 2 * rows, part)]
    unnamed x19 -> x0, local copies, waits for them, and re-layouts: 3.2 us -> none
  transfers between devices with their start and end apart: 6 -> 0, of which waited for: 0 -> 0; matrix products, arithmetic and copies ran while one was open for 8% -> 0% of each run, Pallas kernels for 35% -> 0%
where the time goes in v1:
time: 117 us
  Pallas kernels  116 us (99%)
    pallas_call x1, Pallas kernels, fused(): pl.pallas_call(functools.partial(fused_kernel, rows, cols, heads, blocks)...  110 us
    pallas_call x1, Pallas kernels, unpack(): pl.pallas_call(functools.partial(unpack_kernel, groups), grid=(heads // 2...  5.98 us

profile of v1, /device:TPU:1, one launch (start us, length us, event | category | flops | bytes accessed | tf_op | source)
XLA Modules:
  0.0 116.8 jit_solution(9234309086159935126)
XLA Ops:
  0.6 110.2 %head_attention.1 = (bf16[16,256,128]{2,1,0:T(8,128)(2,1)}, bf16[16,2,128,128]{3,2,1,0:T(8,128)(2,1)}) custom-call(bf16[256,1024]{1,0:T(8,128)(2,1)} %q_ref.1, bf16[256,1024]{1,0:T(8,128)(2,1)} %k_ref.1, bf16[256,1024]{1,0:T(8,128)(2,1)} %v_ref.1, bf16[256,1024]{1,0:T(8,128)(2,1)} %g_ref.1, s32[256,128]{1,0:T(8,128)} %bits_ref.1, s32[3,2,16]{2,1,0:T(2,128)} %partner_ref.1, ...), custom_call_target="tpu_custom_call" | custom-call | tf_op jit(solution)/shard_map/head_attention/pallas_call | solution.py:425
  110.8 6.0 %unpack_heads.1 = (bf16[256,1024]{1,0:T(8,128)(2,1)}, bf16[256,1024]{1,0:T(8,128)(2,1)}, bf16[256,1024]{1,0:T(8,128)(2,1)}, bf16[256,1024]{1,0:T(8,128)(2,1)}) custom-call(bf16[16,256,128]{2,1,0:T(8,128)(2,1)} %get-tuple-element.6.qa_ref, bf16[1,16,256,128]{3,2,1,0:T(8,128)(2,1)} %bitcast.1), custom_call_target="tpu_custom_call" | custom-call | tf_op jit(solution)/shard_map/unpack_heads/pallas_call | solution.py:465

commit v2 on v1

--- a/solution.py
+++ b/solution.py
@@ -12,7 +12,6 @@
 NGLOBAL = 2
 NMATCH = 3
 PAIR = 2 * HEAD_DIM
-SLOTS = 3 + NGLOBAL + NMATCH
 
 score_scale = 0.125
 keep_scale = 1.0 / 0.9
@@ -31,7 +30,7 @@
     q_ref, k_ref, v_ref, g_ref, bits_ref, partner_ref, pick_ref, global_ref,
     qa_land, kvg_land,
     kv_pack, qg_pack, kv_in, qg_in, bits_all, kv_ext, kv_turned, halo, shared, shared_turned,
-    shared_keys, words_ref, s_ref, dsp_ref, acc_ref, rand_ref, gacc_ref, halo_acc, gacc_in, qa_out, kvg_out, inverse_ref,
+    shared_keys, words_ref, s_ref, u_ref, p_ref, ds_ref, acc_ref, rand_ref, gacc_ref, halo_acc, gacc_in, qa_out, kvg_out, inverse_ref,
     kv_send, kv_recv, qg_send, qg_recv, bit_send, bit_recv, row_send, row_recv, back_send, back_recv, qa_send, qa_recv, kvg_send, kvg_recv,
 ):
     me, band = lax.axis_index("col"), lax.axis_index("row")
@@ -212,68 +211,85 @@
         where_bits = tuple((slot // 2 ** (levels - 1 - d)) % 2 for d in range(levels))
         words_ref[slot] = bits_all[where_bits].astype(jnp.float32).astype(jnp.int32)
 
-    wide = 2 * BLOCK
+    wide = blocks * BLOCK
+    reach = blocks + 2
     marks = jnp.left_shift(1, lax.broadcasted_iota(jnp.int32, (BLOCK // 8, 8, BLOCK), 1))
+    p_ref[...] = jnp.zeros_like(p_ref)
+    ds_ref[...] = jnp.zeros_like(ds_ref)
+    first_all = lax.broadcasted_iota(jnp.int32, (wide, PAIR), 1) < HEAD_DIM
+    zero_all = jnp.zeros((wide, PAIR), jnp.bfloat16)
 
     def attend(turn):
         slot = (head + turn * (heads - stride_of(heads))) % heads
         place = group * heads + slot
         far = [1 + partner_ref[r, band, place] * blocks + pick_ref[r, band, place] for r in range(NMATCH)]
-        far_keys = [shared_keys[n] for n in range(NGLOBAL)] + [kv_ext[b] for b in far]
-        near_keys = [kv_ext[place * blocks + b] for b in range(blocks + 2)]
-        sides = []
-        for j in range(blocks):
-            packed = qg_in[turn, j * BLOCK : (j + 1) * BLOCK, :]
-            side = jnp.concatenate([jnp.where(first, packed, zero), jnp.where(first, zero, packed)], axis=0)
-            sides.append(side)
-            keys = near_keys[j : j + 3] + far_keys
-            top = None
-            for i in range(SLOTS):
-                both = contract(keys[i], side, 1, 1)
-                s_ref[i] = both
-                part = jnp.max(both[:, :BLOCK].reshape(BLOCK // 8, 8, BLOCK), axis=0)
-                top = part if top is None else jnp.maximum(top, part)
-            top = jnp.max(top, axis=0, keepdims=True)
-            total, mixed = None, None
-            for i in range(SLOTS):
+        keys = [kv_ext[place * blocks + b] for b in range(reach)]
+        keys += [shared_keys[n] for n in range(NGLOBAL)] + [kv_ext[b] for b in far]
+        seen = [[(j, b - j) for j in range(blocks) if 0 <= b - j < 3] for b in range(reach)]
+        seen += [[(j, 3 + f) for j in range(blocks)] for f in range(NGLOBAL + NMATCH)]
+        packed = qg_in[turn]
+        side_q = jnp.where(first_all, packed, zero_all)
+        side_g = jnp.where(first_all, zero_all, packed)
+        tops = [None] * blocks
+        for b, pairs in enumerate(seen):
+            lower, upper = pairs[0][0] * BLOCK, (pairs[-1][0] + 1) * BLOCK
+            score = contract(keys[b], side_q[lower:upper], 1, 1)
+            s_ref[b, :, lower:upper] = score
+            for j, _ in pairs:
+                tile = score[:, j * BLOCK - lower : (j + 1) * BLOCK - lower]
+                part = jnp.max(tile.reshape(BLOCK // 8, 8, BLOCK), axis=0)
+                tops[j] = part if tops[j] is None else jnp.maximum(tops[j], part)
+        tops = [jnp.max(top, axis=0, keepdims=True) for top in tops]
+        totals, mixed = [0.0] * blocks, [0.0] * blocks
+        for b, pairs in enumerate(seen):
+            lower, upper = pairs[0][0] * BLOCK, (pairs[-1][0] + 1) * BLOCK
+            grad_p = contract(keys[b], side_g[lower:upper], 1, 1)
+            for j, i in pairs:
+                cols_j = slice(j * BLOCK, (j + 1) * BLOCK)
                 words = words_ref[slot, j, i * BLOCK // 8 : (i + 1) * BLOCK // 8, :]
                 keep = (jnp.broadcast_to(words[:, None, :], marks.shape) & marks) != 0
-                weight = jnp.exp(s_ref[i, :, :BLOCK] - top).reshape(marks.shape)
-                grad_p = jnp.where(keep, s_ref[i, :, BLOCK:].reshape(marks.shape), 0.0)
-                s_ref[i, :, :BLOCK] = weight.reshape(BLOCK, BLOCK)
-                s_ref[i, :, BLOCK:] = grad_p.reshape(BLOCK, BLOCK)
-                part = jnp.sum(weight, axis=0)
-                cross = jnp.sum(weight * grad_p, axis=0)
-                total = part if total is None else total + part
-                mixed = cross if mixed is None else mixed + cross
-            inverse = 1.0 / jnp.sum(total, axis=0, keepdims=True)
-            delta = jnp.sum(mixed, axis=0, keepdims=True) * inverse
-            scaled = inverse * keep_scale
-            for i in range(SLOTS):
-                words = words_ref[slot, j, i * BLOCK // 8 : (i + 1) * BLOCK // 8, :]
-                keep = (jnp.broadcast_to(words[:, None, :], marks.shape) & marks) != 0
-                probs = s_ref[i, :, :BLOCK] * scaled
-                dscore = probs * (s_ref[i, :, BLOCK:] - delta)
-                dropped = jnp.where(keep, probs.reshape(marks.shape), 0.0).reshape(BLOCK, BLOCK)
-                dsp_ref[j, i, :, :BLOCK] = dscore.astype(jnp.bfloat16)
-                dsp_ref[j, i, :, BLOCK:] = dropped.astype(jnp.bfloat16)
-            turned = [kv_turned[place * blocks + j + b] for b in range(3)]
-            turned += [shared_turned[n] for n in range(NGLOBAL)] + [kv_turned[b] for b in far]
-            out = contract(jnp.concatenate(turned, axis=1), dsp_ref[j].reshape(SLOTS * BLOCK, wide), 1, 0)
-            out = jnp.concatenate([out[:HEAD_DIM, :BLOCK] * score_scale, out[HEAD_DIM:, BLOCK:]], axis=0)
-            qa_out[turn, j * BLOCK : (j + 1) * BLOCK, :] = out.T.astype(jnp.bfloat16)
+                weight = jnp.exp(s_ref[b, :, cols_j] - tops[j]).reshape(marks.shape)
+                kept = jnp.where(keep, weight, 0.0)
+                cross = kept * grad_p[:, j * BLOCK - lower : (j + 1) * BLOCK - lower].reshape(marks.shape)
+                s_ref[b, :, cols_j] = weight.reshape(BLOCK, BLOCK)
+                u_ref[b, :, cols_j] = cross.reshape(BLOCK, BLOCK)
+                p_ref[b, :, cols_j] = kept.reshape(BLOCK, BLOCK).astype(jnp.bfloat16)
+                totals[j] = totals[j] + jnp.sum(weight, axis=0)
+                mixed[j] = mixed[j] + jnp.sum(cross, axis=0)
+        scales, deltas = [], []
         for j in range(blocks):
-            grads = contract(dsp_ref[j, :3].reshape(3 * BLOCK, wide), sides[j], 1, 0)
-            for b in range(3):
-                acc_ref[place * blocks + j + b] += grads[b * BLOCK : (b + 1) * BLOCK]
-        grads = None
+            inverse = 1.0 / jnp.sum(totals[j], axis=0, keepdims=True)
+            deltas.append(jnp.sum(mixed[j], axis=0, keepdims=True) * inverse)
+            scales.append(inverse * keep_scale)
+        for b, pairs in enumerate(seen):
+            for j, _ in pairs:
+                cols_j = slice(j * BLOCK, (j + 1) * BLOCK)
+                ds_ref[b, :, cols_j] = (u_ref[b, :, cols_j] - s_ref[b, :, cols_j] * deltas[j]).astype(jnp.bfloat16)
+        turned = [kv_turned[place * blocks + b] for b in range(reach)]
+        turned += [shared_turned[n] for n in range(NGLOBAL)] + [kv_turned[b] for b in far]
+        turned = jnp.concatenate(turned, axis=1)
+        whole = (reach + NGLOBAL + NMATCH) * BLOCK
+        out_p = contract(turned, p_ref[...].reshape(whole, wide), 1, 0)
+        out_s = contract(turned, ds_ref[...].reshape(whole, wide), 1, 0)
+        factors = []
         for j in range(blocks):
-            part = contract(dsp_ref[j, 3:].reshape((SLOTS - 3) * BLOCK, wide), sides[j], 1, 0)
-            grads = part if grads is None else grads + part
+            cols_j = slice(j * BLOCK, (j + 1) * BLOCK)
+            out = jnp.concatenate(
+                [out_s[:HEAD_DIM, cols_j] * (scales[j] * score_scale), out_p[HEAD_DIM:, cols_j] * scales[j]], axis=0
+            )
+            qa_out[turn, cols_j, :] = out.T.astype(jnp.bfloat16)
+            factors.append(jnp.broadcast_to(scales[j], (BLOCK, BLOCK)).T)
+        scaled = (packed.astype(jnp.float32) * jnp.concatenate(factors, axis=0)).astype(jnp.bfloat16)
+        grads = contract(ds_ref[...].reshape(whole, wide), jnp.where(first_all, scaled, zero_all), 1, 0)
+        grads = grads + contract(p_ref[...].reshape(whole, wide), jnp.where(first_all, zero_all, scaled), 1, 0)
+        for b in range(reach):
+            acc_ref[place * blocks + b] += grads[b * BLOCK : (b + 1) * BLOCK]
+        base = reach * BLOCK
         for n in range(NGLOBAL):
-            gacc_ref[n] += grads[n * BLOCK : (n + 1) * BLOCK]
+            gacc_ref[n] += grads[base + n * BLOCK : base + (n + 1) * BLOCK]
+        base += NGLOBAL * BLOCK
         for r in range(NMATCH):
-            rand_ref[slot, r] = grads[(NGLOBAL + r) * BLOCK : (NGLOBAL + r + 1) * BLOCK]
+            rand_ref[slot, r] = grads[base + r * BLOCK : base + (r + 1) * BLOCK]
 
     def qa_copy(turn):
         step = (turn * stride_of(heads)) % heads
@@ -392,6 +408,7 @@
     heads = width // HEAD_DIM
     levels = heads.bit_length() - 1
     last = cols * blocks
+    tiles = blocks + 2 + NGLOBAL + NMATCH
     half, full = jnp.bfloat16, jnp.float32
     vmem = pl.BlockSpec(memory_space=pltpu.VMEM)
     smem = pl.BlockSpec(memory_space=pltpu.SMEM)
@@ -409,8 +426,10 @@
         pltpu.VMEM((NGLOBAL, PAIR, BLOCK), half),
         pltpu.VMEM((NGLOBAL, BLOCK, PAIR), half),
         pltpu.VMEM((heads, blocks, BLOCK, BLOCK), jnp.int32),
-        pltpu.VMEM((SLOTS, BLOCK, 2 * BLOCK), full),
-        pltpu.VMEM((blocks, SLOTS, BLOCK, 2 * BLOCK), half),
+        pltpu.VMEM((tiles, BLOCK, tokens_here), full),
+        pltpu.VMEM((tiles, BLOCK, tokens_here), full),
+        pltpu.VMEM((tiles, BLOCK, tokens_here), half),
+        pltpu.VMEM((tiles, BLOCK, tokens_here), half),
         pltpu.VMEM((last + 2, BLOCK, PAIR), full),
         pltpu.VMEM((heads, NMATCH, BLOCK, PAIR), full),
         pltpu.VMEM((NGLOBAL, BLOCK, PAIR), full),
@@ -443,31 +462,34 @@
         high = jnp.concatenate([left[:, HEAD_DIM:], right[:, HEAD_DIM:]], axis=1)
         return low, high
 
-    qg_ref[...], att_ref[...] = split([qa_ref[0], qa_ref[1]])
-    totals = []
-    for side in range(2):
-        total = kvg_ref[0, side]
-        if groups > 1:
-            total = total.astype(jnp.float32)
-            for g in range(1, groups):
-                total = total + kvg_ref[g, side].astype(jnp.float32)
-            total = total.astype(jnp.bfloat16)
-        totals.append(total)
-    kg_ref[...], vg_ref[...] = split(totals)
+    for p in range(qa_ref.shape[0] // 2):
+        lanes = slice(p * PAIR, (p + 1) * PAIR)
+        qg_ref[:, lanes], att_ref[:, lanes] = split([qa_ref[2 * p], qa_ref[2 * p + 1]])
+        totals = []
+        for side in range(2 * p, 2 * p + 2):
+            total = kvg_ref[0, side]
+            if groups > 1:
+                total = total.astype(jnp.float32)
+                for g in range(1, groups):
+                    total = total + kvg_ref[g, side].astype(jnp.float32)
+                total = total.astype(jnp.bfloat16)
+            totals.append(total)
+        kg_ref[:, lanes], vg_ref[:, lanes] = split(totals)
 
 
 def unpack(qa, kvg):
     heads, tokens_here, _ = qa.shape
     groups = kvg.shape[0] // heads
     kvg = kvg.reshape(groups, heads, tokens_here, PAIR)
-    flat = pl.BlockSpec((tokens_here, PAIR), lambda p: (0, p))
+    rows = tokens_here // 2
+    flat = pl.BlockSpec((rows, heads * HEAD_DIM), lambda t: (t, 0))
     shape = jax.ShapeDtypeStruct((tokens_here, heads * HEAD_DIM), jnp.bfloat16)
     return pl.pallas_call(
         functools.partial(unpack_kernel, groups),
-        grid=(heads // 2,),
+        grid=(2,),
         in_specs=[
-            pl.BlockSpec((2, tokens_here, PAIR), lambda p: (p, 0, 0)),
-            pl.BlockSpec((groups, 2, tokens_here, PAIR), lambda p: (0, p, 0, 0)),
+            pl.BlockSpec((heads, rows, PAIR), lambda t: (0, t, 0)),
+            pl.BlockSpec((groups, heads, rows, PAIR), lambda t: (0, 0, t, 0)),
         ],
         out_specs=[flat] * 4,
         out_shape=[shape] * 4,

time: 117 us -> 112 us (0.957)
  Pallas kernels: 116 us -> 111 us
    pallas_call x1, Pallas kernels: 5.98 us -> 2.94 us  [unpack(): pl.pallas_call(functools.partial(unpack_kernel, groups), grid=(2,), in_sp...]
    pallas_call x1, Pallas kernels: 110 us -> 108 us  [fused(): pl.pallas_call(functools.partial(fused_kernel, rows, cols, heads, blocks)...]
where the time goes in v2:
time: 112 us
  Pallas kernels  111 us (99%)
    pallas_call x1, Pallas kernels, fused(): pl.pallas_call(functools.partial(fused_kernel, rows, cols, heads, blocks)...  108 us
    pallas_call x1, Pallas kernels, unpack(): pl.pallas_call(functools.partial(unpack_kernel, groups), grid=(2,), in_sp...  2.94 us

profile of v2, /device:TPU:1, one launch (start us, length us, event | category | flops | bytes accessed | tf_op | source)
XLA Modules:
  0.0 111.9 jit_solution(14937730531060736101)
XLA Ops:
  0.6 108.3 %head_attention.1 = (bf16[16,256,128]{2,1,0:T(8,128)(2,1)}, bf16[16,2,128,128]{3,2,1,0:T(8,128)(2,1)}) custom-call(bf16[256,1024]{1,0:T(8,128)(2,1)} %q_ref.1, bf16[256,1024]{1,0:T(8,128)(2,1)} %k_ref.1, bf16[256,1024]{1,0:T(8,128)(2,1)} %v_ref.1, bf16[256,1024]{1,0:T(8,128)(2,1)} %g_ref.1, s32[256,128]{1,0:T(8,128)} %bits_ref.1, s32[3,2,16]{2,1,0:T(2,128)} %partner_ref.1, ...), custom_call_target="tpu_custom_call" | custom-call | tf_op jit(solution)/shard_map/head_attention/pallas_call | solution.py:444
  108.9 2.9 %unpack_heads.1 = (bf16[256,1024]{1,0:T(8,128)(2,1)}, bf16[256,1024]{1,0:T(8,128)(2,1)}, bf16[256,1024]{1,0:T(8,128)(2,1)}, bf16[256,1024]{1,0:T(8,128)(2,1)}) custom-call(bf16[16,256,128]{2,1,0:T(8,128)(2,1)} %get-tuple-element.6.qa_ref, bf16[1,16,256,128]{3,2,1,0:T(8,128)(2,1)} %bitcast.1), custom_call_target="tpu_custom_call" | custom-call | tf_op jit(solution)/shard_map/unpack_heads/pallas_call | solution.py:487

commit v3 on v2

--- a/solution.py
+++ b/solution.py
@@ -27,11 +27,11 @@
 
 def fused_kernel(
     rows, cols, heads, blocks,
-    q_ref, k_ref, v_ref, g_ref, bits_ref, partner_ref, pick_ref, global_ref,
+    q_hbm, k_hbm, v_hbm, g_hbm, bits_hbm, partner_ref, pick_ref, global_ref,
     qa_land, kvg_land,
-    kv_pack, qg_pack, kv_in, qg_in, bits_all, kv_ext, kv_turned, halo, shared, shared_turned,
+    q_ref, k_ref, v_ref, g_ref, bits_ref, kv_pack, qg_pack, kv_in, qg_in, bits_all, kv_ext, kv_turned, halo, shared, shared_turned,
     shared_keys, words_ref, s_ref, u_ref, p_ref, ds_ref, acc_ref, rand_ref, gacc_ref, halo_acc, gacc_in, qa_out, kvg_out, inverse_ref,
-    kv_send, kv_recv, qg_send, qg_recv, bit_send, bit_recv, row_send, row_recv, back_send, back_recv, qa_send, qa_recv, kvg_send, kvg_recv,
+    kv_send, kv_recv, qg_send, qg_recv, bit_send, bit_recv, row_send, row_recv, back_send, back_recv, qa_send, qa_recv, kvg_send, kvg_recv, load_sems, own_sems,
 ):
     me, band = lax.axis_index("col"), lax.axis_index("row")
     head, group = me % heads, me // heads
@@ -40,6 +40,14 @@
     first = lax.broadcasted_iota(jnp.int32, (BLOCK, PAIR), 1) < HEAD_DIM
     zero = jnp.zeros((BLOCK, PAIR), jnp.bfloat16)
 
+    load_k, load_v, load_bits, load_q, load_g = [
+        pltpu.make_async_copy(source, target, load_sems.at[n])
+        for n, (source, target) in enumerate(
+            ((k_hbm, k_ref), (v_hbm, v_ref), (bits_hbm, bits_ref), (q_hbm, q_ref), (g_hbm, g_ref))
+        )
+    ]
+    for load in (load_k, load_v, load_bits, load_q, load_g):
+        load.start()
     barrier = pltpu.get_barrier_semaphore()
 
     def hello(step, carry):
@@ -50,6 +58,8 @@
     for step in range(1, rows):
         pl.semaphore_signal(barrier, inc=1, device_id={"row": (band + step) % rows})
 
+    load_k.wait()
+    load_v.wait()
     for p in range(heads // 2):
         lanes = slice(p * PAIR, (p + 1) * PAIR)
         keys, values = k_ref[:, lanes], v_ref[:, lanes]
@@ -59,6 +69,7 @@
         kv_pack[2 * p + 1] = right.reshape(blocks, BLOCK, PAIR)
     flags = [(me // 2 ** (levels - 1 - d)) % 2 for d in range(levels)]
     here = tuple(pl.ds(flag, 1) for flag in flags)
+    load_bits.wait()
     for j in range(blocks):
         words = bits_ref[j * BLOCK : (j + 1) * BLOCK, :].astype(jnp.float32).T.astype(jnp.bfloat16)
         bits_all[here + (j,)] = words.reshape((1,) * levels + words.shape)
@@ -98,6 +109,8 @@
         copy.start()
         lax.fori_loop(bounds[dim], bounds[dim + 1], kv_start, 0)
         if dim == 0:
+            load_q.wait()
+            load_g.wait()
             for p in range(heads // 2):
                 lanes = slice(p * PAIR, (p + 1) * PAIR)
                 query = (q_ref[:, lanes].astype(jnp.float32) * score_scale).astype(jnp.bfloat16)
@@ -310,7 +323,8 @@
 
     attend(0)
     lax.fori_loop(1, heads, segment, 0)
-    qa_land[head] = qa_out[0]
+    own_qa = pltpu.make_async_copy(qa_out.at[0], qa_land.at[head], own_sems.at[0])
+    own_qa.start()
 
     def back_copies():
         copies = [
@@ -387,7 +401,8 @@
 
     lax.fori_loop(1, cols, give, 0)
     collect(0)
-    kvg_land[me] = kvg_out[0]
+    own_kvg = pltpu.make_async_copy(kvg_out.at[0], kvg_land.at[me], own_sems.at[1])
+    own_kvg.start()
 
     def qa_finish(turn, carry):
         qa_copy(turn).wait()
@@ -400,6 +415,8 @@
         return carry
 
     lax.fori_loop(1, cols, kvg_finish, 0)
+    own_qa.wait()
+    own_kvg.wait()
 
 
 def fused(rows, cols, queries, key_rows, value_rows, out_grad, bits, partner, pick, shared_ids):
@@ -410,10 +427,11 @@
     last = cols * blocks
     tiles = blocks + 2 + NGLOBAL + NMATCH
     half, full = jnp.bfloat16, jnp.float32
-    vmem = pl.BlockSpec(memory_space=pltpu.VMEM)
+    anywhere = pl.BlockSpec(memory_space=pl.ANY)
     smem = pl.BlockSpec(memory_space=pltpu.SMEM)
 
-    scratch = [
+    scratch = [pltpu.VMEM((tokens_here, width), half)] * 4 + [pltpu.VMEM(bits.shape, bits.dtype)]
+    scratch += [
         pltpu.VMEM((heads, blocks, BLOCK, PAIR), half),
         pltpu.VMEM((heads, tokens_here, PAIR), half),
         pltpu.VMEM((cols, blocks, BLOCK, PAIR), half),
@@ -441,14 +459,15 @@
     ]
     for count in (cols, heads, levels, rows + 1, rows + 1, heads, cols):
         scratch += [pltpu.SemaphoreType.DMA((count,))] * 2
+    scratch += [pltpu.SemaphoreType.DMA((5,)), pltpu.SemaphoreType.DMA((2,))]
     return pl.pallas_call(
         functools.partial(fused_kernel, rows, cols, heads, blocks),
         out_shape=[
             jax.ShapeDtypeStruct((heads, tokens_here, PAIR), half),
             jax.ShapeDtypeStruct((cols, blocks, BLOCK, PAIR), half),
         ],
-        in_specs=[vmem] * 5 + [smem] * 3,
-        out_specs=[vmem, vmem],
+        in_specs=[anywhere] * 5 + [smem] * 3,
+        out_specs=[anywhere, anywhere],
         scratch_shapes=scratch,
         compiler_params=pltpu.CompilerParams(collective_id=1, has_side_effects=True),
         name="head_attention",

time: 112 us -> 110 us (0.982)
  Pallas kernels: 111 us -> 109 us
    pallas_call x1, Pallas kernels: 108 us -> 106 us  [fused(): pl.pallas_call(functools.partial(fused_kernel, rows, cols, heads, blocks)...]
where the time goes in v3:
time: 110 us
  Pallas kernels  109 us (99%)
    pallas_call x1, Pallas kernels, fused(): pl.pallas_call(functools.partial(fused_kernel, rows, cols, heads, blocks)...  106 us
    pallas_call x1, Pallas kernels, unpack(): pl.pallas_call(functools.partial(unpack_kernel, groups), grid=(2,), in_sp...  2.94 us

profile of v3, /device:TPU:1, one launch (start us, length us, event | category | flops | bytes accessed | tf_op | source)
XLA Modules:
  0.0 110.0 jit_solution(13382393796825174454)
XLA Ops:
  0.6 106.4 %head_attention.1 = (bf16[16,256,128]{2,1,0:T(8,128)(2,1)}, bf16[16,2,128,128]{3,2,1,0:T(8,128)(2,1)}) custom-call(bf16[256,1024]{1,0:T(8,128)(2,1)} %q_hbm.1, bf16[256,1024]{1,0:T(8,128)(2,1)} %k_hbm.1, bf16[256,1024]{1,0:T(8,128)(2,1)} %v_hbm.1, bf16[256,1024]{1,0:T(8,128)(2,1)} %g_hbm.1, s32[256,128]{1,0:T(8,128)} %bits_hbm.1, s32[3,2,16]{2,1,0:T(2,128)} %partner_ref.1, ...), custom_call_target="tpu_custom_call" | custom-call | tf_op jit(solution)/shard_map/head_attention/pallas_call | solution.py:463
  107.0 2.9 %unpack_heads.1 = (bf16[256,1024]{1,0:T(8,128)(2,1)}, bf16[256,1024]{1,0:T(8,128)(2,1)}, bf16[256,1024]{1,0:T(8,128)(2,1)}, bf16[256,1024]{1,0:T(8,128)(2,1)}) custom-call(bf16[16,256,128]{2,1,0:T(8,128)(2,1)} %get-tuple-element.6.qa_ref, bf16[1,16,256,128]{3,2,1,0:T(8,128)(2,1)} %bitcast.1), custom_call_target="tpu_custom_call" | custom-call | tf_op jit(solution)/shard_map/unpack_heads/pallas_call | solution.py:506

commit v4 on v3

--- a/solution.py
+++ b/solution.py
@@ -153,6 +153,12 @@
 
     lax.fori_loop(0, last + 2, clear, 0)
     gacc_ref[...] = jnp.zeros_like(gacc_ref)
+    p_ref[...] = jnp.zeros_like(p_ref)
+    ds_ref[...] = jnp.zeros_like(ds_ref)
+    for slot in range(heads):
+        where_bits = tuple((slot // 2 ** (levels - 1 - d)) % 2 for d in range(levels))
+        words_ref[slot] = bits_all[where_bits].astype(jnp.float32).astype(jnp.int32)
+
 
     def turn_block(value):
         return value.astype(jnp.float32).T.astype(jnp.bfloat16)
@@ -220,15 +226,9 @@
         shared_keys[n] = value
         shared_turned[n] = turn_block(value)
 
-    for slot in range(heads):
-        where_bits = tuple((slot // 2 ** (levels - 1 - d)) % 2 for d in range(levels))
-        words_ref[slot] = bits_all[where_bits].astype(jnp.float32).astype(jnp.int32)
-
     wide = blocks * BLOCK
     reach = blocks + 2
     marks = jnp.left_shift(1, lax.broadcasted_iota(jnp.int32, (BLOCK // 8, 8, BLOCK), 1))
-    p_ref[...] = jnp.zeros_like(p_ref)
-    ds_ref[...] = jnp.zeros_like(ds_ref)
     first_all = lax.broadcasted_iota(jnp.int32, (wide, PAIR), 1) < HEAD_DIM
     zero_all = jnp.zeros((wide, PAIR), jnp.bfloat16)
 
@@ -274,35 +274,40 @@
             inverse = 1.0 / jnp.sum(totals[j], axis=0, keepdims=True)
             deltas.append(jnp.sum(mixed[j], axis=0, keepdims=True) * inverse)
             scales.append(inverse * keep_scale)
-        for b, pairs in enumerate(seen):
-            for j, _ in pairs:
-                cols_j = slice(j * BLOCK, (j + 1) * BLOCK)
-                ds_ref[b, :, cols_j] = (u_ref[b, :, cols_j] - s_ref[b, :, cols_j] * deltas[j]).astype(jnp.bfloat16)
         turned = [kv_turned[place * blocks + b] for b in range(reach)]
         turned += [shared_turned[n] for n in range(NGLOBAL)] + [kv_turned[b] for b in far]
         turned = jnp.concatenate(turned, axis=1)
         whole = (reach + NGLOBAL + NMATCH) * BLOCK
         out_p = contract(turned, p_ref[...].reshape(whole, wide), 1, 0)
+        factors = jnp.concatenate([jnp.broadcast_to(scales[j], (BLOCK, BLOCK)).T for j in range(blocks)], axis=0)
+        scaled = (packed.astype(jnp.float32) * factors).astype(jnp.bfloat16)
+
+        def gather(grads):
+            for b in range(reach):
+                acc_ref[place * blocks + b] += grads[b * BLOCK : (b + 1) * BLOCK]
+            base = reach * BLOCK
+            for n in range(NGLOBAL):
+                gacc_ref[n] += grads[base + n * BLOCK : base + (n + 1) * BLOCK]
+            base += NGLOBAL * BLOCK
+            return [grads[base + r * BLOCK : base + (r + 1) * BLOCK] for r in range(NMATCH)]
+
+        picked = gather(contract(p_ref[...].reshape(whole, wide), jnp.where(first_all, zero_all, scaled), 1, 0))
+        for r in range(NMATCH):
+            rand_ref[slot, r] = picked[r]
+        for b, pairs in enumerate(seen):
+            for j, _ in pairs:
+                cols_j = slice(j * BLOCK, (j + 1) * BLOCK)
+                ds_ref[b, :, cols_j] = (u_ref[b, :, cols_j] - s_ref[b, :, cols_j] * deltas[j]).astype(jnp.bfloat16)
         out_s = contract(turned, ds_ref[...].reshape(whole, wide), 1, 0)
-        factors = []
         for j in range(blocks):
             cols_j = slice(j * BLOCK, (j + 1) * BLOCK)
             out = jnp.concatenate(
                 [out_s[:HEAD_DIM, cols_j] * (scales[j] * score_scale), out_p[HEAD_DIM:, cols_j] * scales[j]], axis=0
             )
             qa_out[turn, cols_j, :] = out.T.astype(jnp.bfloat16)
-            factors.append(jnp.broadcast_to(scales[j], (BLOCK, BLOCK)).T)
-        scaled = (packed.astype(jnp.float32) * jnp.concatenate(factors, axis=0)).astype(jnp.bfloat16)
-        grads = contract(ds_ref[...].reshape(whole, wide), jnp.where(first_all, scaled, zero_all), 1, 0)
-        grads = grads + contract(p_ref[...].reshape(whole, wide), jnp.where(first_all, zero_all, scaled), 1, 0)
-        for b in range(reach):
-            acc_ref[place * blocks + b] += grads[b * BLOCK : (b + 1) * BLOCK]
-        base = reach * BLOCK
-        for n in range(NGLOBAL):
-            gacc_ref[n] += grads[base + n * BLOCK : base + (n + 1) * BLOCK]
-        base += NGLOBAL * BLOCK
+        picked = gather(contract(ds_ref[...].reshape(whole, wide), jnp.where(first_all, scaled, zero_all), 1, 0))
         for r in range(NMATCH):
-            rand_ref[slot, r] = grads[base + r * BLOCK : base + (r + 1) * BLOCK]
+            rand_ref[slot, r] += picked[r]
 
     def qa_copy(turn):
         step = (turn * stride_of(heads)) % heads

time: 110 us -> 109 us (level)
  no operation moved by 1% of the time
where the time goes in v4:
time: 109 us
  Pallas kernels  108 us (99%)
    pallas_call x1, Pallas kernels, fused(): pl.pallas_call(functools.partial(fused_kernel, rows, cols, heads, blocks)...  106 us
    pallas_call x1, Pallas kernels, unpack(): pl.pallas_call(functools.partial(unpack_kernel, groups), grid=(2,), in_sp...  2.94 us

profile of v4, /device:TPU:1, one launch (start us, length us, event | category | flops | bytes accessed | tf_op | source)
XLA Modules:
  0.0 109.1 jit_solution(7144437300953054162)
XLA Ops:
  0.6 105.5 %head_attention.1 = (bf16[16,256,128]{2,1,0:T(8,128)(2,1)}, bf16[16,2,128,128]{3,2,1,0:T(8,128)(2,1)}) custom-call(bf16[256,1024]{1,0:T(8,128)(2,1)} %q_hbm.1, bf16[256,1024]{1,0:T(8,128)(2,1)} %k_hbm.1, bf16[256,1024]{1,0:T(8,128)(2,1)} %v_hbm.1, bf16[256,1024]{1,0:T(8,128)(2,1)} %g_hbm.1, s32[256,128]{1,0:T(8,128)} %bits_hbm.1, s32[3,2,16]{2,1,0:T(2,128)} %partner_ref.1, ...), custom_call_target="tpu_custom_call" | custom-call | tf_op jit(solution)/shard_map/head_attention/pallas_call | solution.py:468
  106.2 2.9 %unpack_heads.1 = (bf16[256,1024]{1,0:T(8,128)(2,1)}, bf16[256,1024]{1,0:T(8,128)(2,1)}, bf16[256,1024]{1,0:T(8,128)(2,1)}, bf16[256,1024]{1,0:T(8,128)(2,1)}) custom-call(bf16[16,256,128]{2,1,0:T(8,128)(2,1)} %get-tuple-element.6.qa_ref, bf16[1,16,256,128]{3,2,1,0:T(8,128)(2,1)} %bitcast.1), custom_call_target="tpu_custom_call" | custom-call | tf_op jit(solution)/shard_map/unpack_heads/pallas_call | solution.py:511
